TPU v7x, 32 devices: a whole 2x2x4 slice. The times are simulated.
32 devices in a mesh: facet: 2 (over y), sub: 16 (over z, x, core).
Axes of the slice: x: 2, y: 2, z: 4, core: 2. Of those that a mesh axis runs over, the one named last changes fastest.
Arguments:
- contributions: bfloat16 [16, 16, 2, 2, 192, 192], P('facet', 'sub'), may hold values from -6 to 6
- slot_subgrid: int32 [16, 2, 2], P('sub'), may hold values from -1 to 1, as said below
- vis_count: int32 [2, 16, 2], P('facet', 'sub'), may hold values from 0 to 384, as said below
- vis_uv: float32 [2, 16, 2, 2, 384], P('facet', 'sub'), may hold values from 0 to 512
- vis_obs: float32 [2, 16, 2, 2, 384], P('facet', 'sub'), may hold values from -6 to 6
- vis_weight: float32 [2, 16, 2, 384], P('facet', 'sub'), may hold values from 0.25 to 2
- subgrid_offset: int32 [16, 2, 2], P('sub'), may hold values from 0 to 511
Outputs:
- facet_residual: float32 [16, 2, 512, 512], P('facet', None, 'sub')
Inputs may be any that keep to these rules, and one draw needn't show every extreme that they name: `slot_subgrid`: in every column each of the 2 subgrids sits in exactly one of the 2 x 2 slots and the other slots hold -1; in every column the 2 slots of some device are all used. `vis_count`: 0 exactly for slots that hold no subgrid, from 384 // 4 to 384 for the others, and 384 in some slot of every column.
All inputs are finite; a program needn't handle non-finite values.
Results may differ from a plain program's by a relative error of at most 0.013.
Values may be sent and summed in bfloat16 or wider, within the bound.
A program may use at most 128 MiB of HBM per device.

v0:
```python
import math

import jax
import jax.numpy as jnp
from jax import lax
from jax.sharding import PartitionSpec as P

SUBGRID = 512
CONTRIB = 192
FACET_SIDE = 4
WIN = 512
VCAP = 384
SG_DEV = 1
FACETS = 16


def corner_cells(facet_index):
    stride = (SUBGRID - CONTRIB) // (FACET_SIDE - 1)
    return (facet_index // FACET_SIDE * stride, facet_index % FACET_SIDE * stride)


def assemble(blocks):
    subgrid_image = None
    for facet_index in range(FACETS):
        start_row, start_column = corner_cells(facet_index)
        padded = jnp.pad(
            blocks[facet_index].astype(jnp.float32),
            (
                (0, 0),
                (start_row, SUBGRID - start_row - CONTRIB),
                (start_column, SUBGRID - start_column - CONTRIB),
            ),
        )
        subgrid_image = padded if subgrid_image is None else subgrid_image + padded
    return subgrid_image.astype(jnp.bfloat16)


def phase_tables(coordinate):
    cell_grid = jnp.arange(SUBGRID, dtype=jnp.float32)
    phase_angle = 2.0 * math.pi / SUBGRID * cell_grid[:, None] * coordinate[None, :]
    return (jnp.cos(phase_angle).astype(jnp.bfloat16), (-jnp.sin(phase_angle)).astype(jnp.bfloat16))


def visit_subgrid(subgrid_image, coordinates, observed, weight, visible_count):
    first_real, first_imaginary = phase_tables(coordinates[0])
    second_real, second_imaginary = phase_tables(coordinates[1])
    cells = SUBGRID
    visits = coordinates.shape[1]
    stacked = jnp.concatenate([subgrid_image[0], subgrid_image[1]], axis=0)
    partial_sums = jnp.dot(
        stacked,
        jnp.concatenate([second_real, second_imaginary], axis=1),
        preferred_element_type=jnp.float32,
    )
    inner_real = partial_sums[:cells, :visits] - partial_sums[cells:, visits:]
    inner_imaginary = partial_sums[:cells, visits:] + partial_sums[cells:, :visits]
    first_rf = first_real.astype(jnp.float32)
    first_if = first_imaginary.astype(jnp.float32)
    model_real = jnp.sum(first_rf * inner_real - first_if * inner_imaginary, axis=0) / SUBGRID
    model_imaginary = jnp.sum(first_rf * inner_imaginary + first_if * inner_real, axis=0) / SUBGRID
    active = jnp.arange(visits) < visible_count
    residual_real = jnp.where(active, weight * (observed[0] - model_real), 0.0).astype(jnp.bfloat16)
    residual_imaginary = jnp.where(active, weight * (observed[1] - model_imaginary), 0.0).astype(
        jnp.bfloat16
    )
    real_float = residual_real.astype(jnp.float32)
    imaginary_float = residual_imaginary.astype(jnp.float32)
    lift_real = (first_rf * real_float + first_if * imaginary_float).astype(jnp.bfloat16)
    lift_imaginary = (first_rf * imaginary_float - first_if * real_float).astype(jnp.bfloat16)
    lifted = jnp.concatenate([lift_real, lift_imaginary], axis=0)
    tables = jnp.concatenate([second_real, second_imaginary], axis=0)
    gridded = lax.dot_general(
        lifted, tables, (((1,), (1,)), ((), ())), preferred_element_type=jnp.float32
    )
    grid_scale = 1.0 / math.sqrt(VCAP)
    grid_real = (gridded[:cells, :cells] + gridded[cells:, cells:]) * grid_scale
    grid_imaginary = (gridded[cells:, :cells] - gridded[:cells, cells:]) * grid_scale
    grid_both = jnp.stack([grid_real, grid_imaginary])
    pieces = []
    for facet_index in range(FACETS):
        start_row, start_column = corner_cells(facet_index)
        pieces.append(
            grid_both[:, start_row : start_row + CONTRIB, start_column : start_column + CONTRIB]
        )
    return jnp.stack(pieces).astype(jnp.bfloat16)


def place_piece(accum, pieces, offset):
    anchor = jnp.zeros((), jnp.int32)
    corner_start = (anchor, anchor, offset[0], offset[1])
    current = lax.dynamic_slice(accum, corner_start, pieces.shape)
    return lax.dynamic_update_slice(accum, current + pieces.astype(jnp.float32), corner_start)


def fold_edges(accum):
    upper = accum[:, :, :WIN].at[:, :, :CONTRIB].add(accum[:, :, WIN:])
    return upper[..., :WIN].at[..., :CONTRIB].add(upper[..., WIN:])


def body(contributions, slot_subgrid, vis_count, vis_uv, vis_obs, vis_weight, subgrid_offset):
    groups = lax.axis_size("facet")
    columns = lax.axis_size("sub")
    facet_here = lax.axis_index("facet")
    per_group = contributions.shape[0]
    slot_table = slot_subgrid[0]
    owned = contributions[:, 0]
    gathered = (
        lax.all_gather(vis_count[0, 0], "facet", axis=0, tiled=True),
        lax.all_gather(vis_uv[0, 0], "facet", axis=0, tiled=True),
        lax.all_gather(vis_obs[0, 0], "facet", axis=0, tiled=True),
        lax.all_gather(vis_weight[0, 0], "facet", axis=0, tiled=True),
    )
    outgoing = owned.reshape((per_group, groups, SG_DEV) + owned.shape[2:])
    arrived = lax.all_to_all(outgoing, "facet", split_axis=1, concat_axis=0, tiled=True)
    arrived = arrived.reshape((groups * per_group, SG_DEV) + owned.shape[2:])
    flattened = slot_table.reshape(-1)
    wanted = facet_here * SG_DEV + 0
    position = jnp.argmax(flattened == wanted)
    subgrid_image = assemble(arrived[:, 0])
    returns_list = [
        visit_subgrid(
            subgrid_image,
            gathered[1][position],
            gathered[2][position],
            gathered[3][position],
            gathered[0][position],
        )
    ]
    returned = jnp.stack(returns_list, axis=1)
    returned = returned.reshape((groups, per_group) + returned.shape[1:])
    homeward = lax.all_to_all(returned, "facet", split_axis=0, concat_axis=0, tiled=True)
    members = (
        jnp.arange(groups, dtype=jnp.int32)[:, None] * SG_DEV
        + jnp.arange(SG_DEV, dtype=jnp.int32)[None, :]
    )
    per_source = members.shape[1]
    padded_width = WIN + CONTRIB
    start_accum = jnp.zeros((per_group, 2, padded_width, padded_width), jnp.float32)

    def settle(position_index, accum):
        source = position_index // per_source
        member_index = position_index % per_source
        subgrid = members[source, member_index]
        return place_piece(accum, homeward[source, :, member_index], subgrid_offset[0, subgrid])

    accum = lax.fori_loop(0, groups * per_source, settle, start_accum)
    window = fold_edges(accum)
    summed = lax.psum_scatter(window, "sub", scatter_dimension=2, tiled=True)
    window_gain = WIN / (CONTRIB * math.sqrt(SG_DEV * groups * columns))
    return summed * window_gain


def solution(mesh):
    placed = (
        P("facet", "sub", None, None, None, None),
        P("sub", None, None),
        P("facet", "sub", None),
        P("facet", "sub", None, None, None),
        P("facet", "sub", None, None, None),
        P("facet", "sub", None, None),
        P("sub", None, None),
    )
    return jax.shard_map(
        body, mesh=mesh, in_specs=placed, out_specs=P("facet", None, "sub", None), check_vma=False
    )
```

profile of v0, /device:TPU:0, one launch (start us, length us, event | category | flops | bytes accessed | tf_op | source)
XLA Modules:
  0.0 500.9 jit_solution(14034782540991081871)
XLA Ops:
  6.5 3.9 copy.17
  10.4 0.0 copy-start.1
  10.4 0.0 copy-start.2
  10.5 4.4 all-to-all-start
  14.9 0.6 dynamic-slice.20
  16.1 0.0 copy-done.6
  16.1 0.1 bitcast_dynamic-update-slice_fusion
  16.2 36.0 %all-reduce.16 = s32[4]{0:T(128)S(1)} all-reduce(s32[4]{0:T(128)S(1)} %bitcast_dynamic-update-slice_fusion), channel_id=3, replica_groups=mesh['facet'=2,'sub'=16] {'facet'}, use_global_device_ids=true, to_apply=%add.16 | all-reduce | flops 4 | bytes 32
  52.2 0.1 eq.17
  52.3 0.6 iota_reduce_fusion
  54.6 0.6 dynamic-slice.21
  55.2 4.5 all-gather.2
  59.7 4.4 all-gather
  64.1 4.4 all-gather.3
  68.5 3.9 fusion.11
  72.3 0.0 all-to-all-done
  72.3 0.3 slice_bitcast_fusion.33
  72.6 0.0 copy-start
  72.7 2.6 add_convert_fusion
  75.3 0.1 slice_bitcast_fusion.1
  75.4 1.0 fusion.4
  76.4 3.5 fusion.15
  79.9 1.3 fusion.50
  81.2 3.4 fusion.17
  84.5 1.3 fusion.25
  85.8 0.6 fusion.3
  86.4 0.1 maximum_convert_fusion
  86.5 0.7 fusion.47
  87.2 0.8 fusion.46
  88.0 0.8 fusion.45
  88.8 0.8 fusion.44
  89.6 0.7 fusion.43
  90.3 0.8 fusion.42
  91.1 0.8 fusion.41
  91.9 0.8 fusion.40
  92.8 0.7 fusion.39
  93.5 0.8 fusion.38
  94.3 0.8 fusion.37
  95.1 0.8 fusion.36
  96.0 0.7 fusion.35
  96.7 0.8 fusion.34
  97.5 0.8 fusion.33
  98.3 0.8 fusion.32
  99.2 5.2 %all-to-all-start.1 = ((bf16[2,8,1,2,192,192]{5,4,3,1,2,0:T(8,128)(2,1)}), bf16[2,8,1,2,192,192]{5,4,3,1,2,0:T(8,128)(2,1)}, u32[]{:S(2)}, u32[]{:S(2)}) async-start(bf16[2,8,1,2,192,192]{5,4,3,1,2,0:T(8,128)(2,1)} %bitcast.57), calls=%async_computation.1 | async-start | bytes 6291456 | tf_op jit(solution)/shard_map/all_to_all | solution.py:131
  104.4 0.2 reduce-scatter.2.cloned.1.call-start
  104.6 32.2 %all-to-all-done.1 = bf16[2,8,1,2,192,192]{5,4,3,1,2,0:T(8,128)(2,1)} async-done(((bf16[2,8,1,2,192,192]{5,4,3,1,2,0:T(8,128)(2,1)}), bf16[2,8,1,2,192,192]{5,4,3,1,2,0:T(8,128)(2,1)}, u32[]{:S(2)}, u32[]{:S(2)}) %all-to-all-start.1) | async-done | bytes 2359328 | tf_op jit(solution)/shard_map/all_to_all | solution.py:131
  136.8 11.4 %broadcast_in_dim.7 = f32[8,2,704,704]{3,2,1,0:T(8,128)} broadcast(f32[]{:T(128)} %constant.149.clone.1), dimensions={} | broadcast | bytes 31719428 | tf_op jit(solution)/shard_map/broadcast_in_dim | solution.py:138
  148.1 73.9 %while.17 = (s32[]{:T(128)}, f32[8,2,704,704]{3,2,1,0:T(8,128)}, s32[2,1]{0,1:T(1,128)S(1)}, s32[1,2,2]{2,1,0:T(2,128)S(1)}, bf16[2,8,1,2,192,192]{5,4,3,1,2,0:T...) while((s32[]{:T(128)}, f32[8,2,704,704]{3,2,1,0:T(8,128)}, s32[2,1]{0,1:T(1,128)S(1)}, ...), condition=%wide.region_4.5_spmd, body=%wide.region_3.4_spmd.sunk | while | flops 1179659 | bytes 10617099 | solution.py:146
  148.1 0.6 constant_dynamic-slice_fusion.5
  150.6 0.6 fusion.62
  154.8 3.8 convert_add_fusion.2
  158.6 27.1 %dynamic_update_slice.11 = f32[8,2,704,704]{3,2,1,0:T(8,128)} dynamic-update-slice(f32[8,2,704,704]{3,2,1,0:T(8,128)} %get-tuple-element.255, f32[8,2,192,192]{3,2,1,0:T(8,128)S(1)} %convert_add_fusion.2, s32[]{:T(128)} %constant.148.clone.1..sunk, s32[]{:T(128)} %constant.148.clone.1..sunk, s32[]{:T(128)S(6)} %select_n.104, s32[]{:T(128)S(6)} %select_n.105) | dynamic-update-slice | bytes 4718596 | tf_op jit(solution)/shard_map/while/body/eval_jaxpr/dynamic_update_slice | solution.py:92
  185.7 0.6 constant_dynamic-slice_fusion.5
  188.1 0.6 fusion.62
  192.3 3.8 convert_add_fusion.2
  196.1 26.0 %dynamic_update_slice.11 = f32[8,2,704,704]{3,2,1,0:T(8,128)} dynamic-update-slice(f32[8,2,704,704]{3,2,1,0:T(8,128)} %get-tuple-element.255, f32[8,2,192,192]{3,2,1,0:T(8,128)S(1)} %convert_add_fusion.2, s32[]{:T(128)} %constant.148.clone.1..sunk, s32[]{:T(128)} %constant.148.clone.1..sunk, s32[]{:T(128)S(6)} %select_n.104, s32[]{:T(128)S(6)} %select_n.105) | dynamic-update-slice | bytes 4718596 | tf_op jit(solution)/shard_map/while/body/eval_jaxpr/dynamic_update_slice | solution.py:92
  222.1 17.1 %slice.298 = f32[8,2,512,704]{3,2,1,0:T(8,128)} slice(f32[8,2,704,704]{3,2,1,0:T(8,128)} %get-tuple-element.165), slice={[0:8], [0:2], [0:512], [0:704]} | slice | bytes 46137344 | tf_op jit(solution)/shard_map/slice | solution.py:96
  239.2 11.4 %add_dynamic-update-slice_fusion = f32[8,2,512,704]{3,2,1,0:T(8,128)} fusion(f32[8,2,512,704]{3,2,1,0:T(8,128)} %slice.298, f32[8,2,704,704]{3,2,1,0:T(8,128)} %get-tuple-element.165), kind=kLoop, calls=%fused_computation.3 | loop fusion | flops 2162688 | bytes 28311552 | tf_op jit(solution)/shard_map/scatter-add | solution.py:96
  250.6 10.4 %slice_add_fusion = f32[8,2,512,192]{3,2,1,0:T(8,128)} fusion(f32[8,2,512,704]{3,2,1,0:T(8,128)} %add_dynamic-update-slice_fusion), kind=kLoop, calls=%fused_computation.4 | loop fusion | flops 1572864 | bytes 18874368 | tf_op jit(solution)/shard_map/add | solution.py:97
  260.9 11.6 %slice.350 = f32[8,2,512,512]{3,2,1,0:T(8,128)} slice(f32[8,2,512,704]{3,2,1,0:T(8,128)} %add_dynamic-update-slice_fusion), slice={[0:8], [0:2], [0:512], [0:512]} | slice | bytes 33554432 | tf_op jit(solution)/shard_map/slice | solution.py:97
  272.5 40.5 %scatter-add.9 = f32[8,2,512,512]{3,2,1,0:T(8,128)} dynamic-update-slice(f32[8,2,512,512]{3,2,1,0:T(8,128)} %slice.350, f32[8,2,512,192]{3,2,1,0:T(8,128)} %slice_add_fusion, s32[]{:T(128)} %constant.148.clone.1, s32[]{:T(128)} %constant.148.clone.1, s32[]{:T(128)} %constant.148.clone.1, s32[]{:T(128)} %constant.148.clone.1) | dynamic-update-slice | bytes 12582916 | tf_op jit(solution)/shard_map/scatter-add | solution.py:97
  313.0 0.0 reduce-scatter.2.cloned.1.call-update
  313.0 178.8 %reduce-scatter.2.cloned.1.call-done = f32[8,2,32,512]{3,2,1,0:T(8,128)} async-done(((f32[8,2,512,512]{3,2,1,0:T(8,128)}), f32[8,2,32,512]{3,2,1,0:T(8,128)}) %reduce-scatter.2.cloned.1.call-update) | async-done | bytes 1048592 | tf_op jit(solution)/shard_map/reduce_scatter | solution.py:148
  491.8 2.3 broadcast_multiply_fusion
  (23 shorter events, 0.1 us)
Async XLA Ops:
  10.4 4.4 copy-start.7
  10.4 5.7 %copy-start.6 = (s32[1,1,2]{2,1,0:T(1,128)S(1)}, s32[1,1,2]{2,1,0:T(1,128)}, u32[]{:S(2)}) copy-start(s32[1,1,2]{2,1,0:T(1,128)} %param.15) | copy-start | bytes 28
  10.4 41.8 %copy-start.4 = (s32[1,2,2]{2,1,0:T(2,128)S(1)}, s32[1,2,2]{2,1,0:T(2,128)}, u32[]{:S(2)}) copy-start(s32[1,2,2]{2,1,0:T(2,128)} %param.14) | copy-start | bytes 52
  10.4 43.6 %copy-start.3 = (f32[1,1,2,384]{3,2,1,0:T(2,128)S(1)}, f32[1,1,2,384]{3,2,1,0:T(2,128)}, u32[]{:S(2)}) copy-start(f32[1,1,2,384]{3,2,1,0:T(2,128)} %param.18) | copy-start | bytes 9220
  10.4 49.2 %copy-start.1 = (f32[1,1,2,2,384]{4,3,2,1,0:T(2,128)S(1)}, f32[1,1,2,2,384]{4,3,2,1,0:T(2,128)}, u32[]{:S(2)}) copy-start(f32[1,1,2,2,384]{4,3,2,1,0:T(2,128)} %param.16) | copy-start | bytes 18436
  10.4 53.6 %copy-start.2 = (f32[1,1,2,2,384]{4,3,2,1,0:T(2,128)S(1)}, f32[1,1,2,2,384]{4,3,2,1,0:T(2,128)}, u32[]{:S(2)}) copy-start(f32[1,1,2,2,384]{4,3,2,1,0:T(2,128)} %param.17) | copy-start | bytes 18436
  10.5 61.9 %all-to-all-start = ((bf16[8,2,1,2,192,192]{5,4,3,0,2,1:T(8,128)(2,1)}), bf16[8,2,1,2,192,192]{5,4,3,0,2,1:T(8,128)(2,1)S(1)}, u32[]{:S(2)}, u32[]{:S(2)}) async-start(bf16[8,2,1,2,192,192]{5,4,3,0,2,1:T(8,128)(2,1)} %bitcast.163), calls=%async_computation | async-start | bytes 6291456 | tf_op jit(solution)/shard_map/all_to_all | solution.py:114
  72.6 2.7 copy-start
  99.2 37.6 %all-to-all-start.1 = ((bf16[2,8,1,2,192,192]{5,4,3,1,2,0:T(8,128)(2,1)}), bf16[2,8,1,2,192,192]{5,4,3,1,2,0:T(8,128)(2,1)}, u32[]{:S(2)}, u32[]{:S(2)}) async-start(bf16[2,8,1,2,192,192]{5,4,3,1,2,0:T(8,128)(2,1)} %bitcast.57), calls=%async_computation.1 | async-start | bytes 6291456 | tf_op jit(solution)/shard_map/all_to_all | solution.py:131
  104.4 387.4 %reduce-scatter.2.cloned.1.call-start = ((), (), s32[]{:S(2)}) async-start(), calls=%async_computation.3 | async-start | bytes 17825792 | tf_op jit(solution)/shard_map/reduce_scatter | solution.py:148
  136.8 11.4 %copy-start.5 = (s32[1,2,2]{2,1,0:T(2,128)S(1)}, s32[1,2,2]{2,1,0:T(2,128)}, u32[]{:S(2)}) copy-start(s32[1,2,2]{2,1,0:T(2,128)} %param.19) | copy-start | bytes 52
Sparse Core Ops, SparseCore 0:
  313.1 178.6 reduce-scatter.1
where the time goes:
time: 504 us; the launch traced here: 501 us
  waiting for transfers between devices  211 us (42%)
  local copies, waits for them, and re-layouts  154 us (31%)
  blocking collectives  49.2 us (10%)
  other arithmetic  47.6 us (9%)
  between operations  15.9 us (3%)
  loops' own time  10.9 us (2%)
  starting transfers between devices  9.81 us (2%)
    reduce_scatter x1, waiting for transfers between devices, body(): summed = lax.psum_scatter(window, 'sub', scatter_dimension=2, tiled=True)  179 us
    dynamic_update_slice x2, local copies, waits for them, and re-layouts, place_piece(): lax.dynamic_update_slice(accum, current + pieces.astype(jnp.float32), cor...  53.1 us
    scatter-add x1, local copies, waits for them, and re-layouts, fold_edges(): return upper[..., :WIN].at[..., :CONTRIB].add(upper[..., WIN:])  40.5 us
    unnamed x1, blocking collectives  36 us
    all_to_all x1, waiting for transfers between devices, body(): lax.all_to_all(returned, 'facet', split_axis=0, concat_axis=0, tiled=True)  32.2 us
    slice x1, local copies, waits for them, and re-layouts, fold_edges(): upper = accum[:, :, :WIN].at[:, :, :CONTRIB].add(accum[:, :, WIN:])  17.1 us
    unnamed x36, local copies, waits for them, and re-layouts  16.5 us
    slice x1, local copies, waits for them, and re-layouts, fold_edges(): return upper[..., :WIN].at[..., :CONTRIB].add(upper[..., WIN:])  11.6 us
  transfers between devices with their start and end apart: 3, of which 2 were waited for; matrix products, arithmetic and copies ran while one was open for 1% of the time, Pallas kernels for 0%

commit v1 on v0

v1 whole, which is shorter than its diff:
```python
import functools
import math

import jax
import jax.numpy as jnp
from jax import lax
from jax.experimental import pallas as pl
from jax.experimental.pallas import tpu as pltpu
from jax.sharding import PartitionSpec as P

SUBGRID = 512
FACET_SIDE = 4
WIN = 512
BLOCK = 16
ALIGNED = 256


def cis(turn):
    turn = turn - jnp.floor(turn + 0.5)
    x = turn * math.pi
    q = x * x
    s = -1.0 / math.factorial(11)
    for order in (9, 7, 5, 3, 1):
        sign = 1.0 if order % 4 == 1 else -1.0
        s = s * q + sign / math.factorial(order)
    s = s * x
    c = 1.0 / math.factorial(12)
    for order in (10, 8, 6, 4, 2, 0):
        sign = 1.0 if order % 4 == 0 else -1.0
        c = c * q + sign / math.factorial(order)
    return 1.0 - 2.0 * s * s, 2.0 * s * c


def turns(k, w):
    high = jnp.floor(w * 4096.0) * (1.0 / 4096.0)
    low = w - high
    p = k * high
    return (p - jnp.floor(p + 0.5)) + k * low


def cmul(a, b):
    return a[0] * b[0] - a[1] * b[1], a[0] * b[1] + a[1] * b[0]


def row_iota(rows, lanes):
    return lax.broadcasted_iota(jnp.int32, (rows, lanes), 0)


def corner(index, stride):
    return lax.div(index, FACET_SIDE) * stride, lax.rem(index, FACET_SIDE) * stride


def partial_models(facet_here, per_group, c_ref, u_of, v_of, put, cs, rhs):
    side = c_ref.shape[-1]
    members = c_ref.shape[1]
    stride = (SUBGRID - side) // (FACET_SIDE - 1)
    across = min(per_group, FACET_SIDE)
    down = per_group // across
    lanes = rhs.shape[1] // 2
    first_row, first_col = corner(facet_here * per_group, stride)
    lines = row_iota(BLOCK, lanes)
    cs[...] = jnp.zeros_like(cs)
    rhs[...] = jnp.zeros_like(rhs)

    @pl.loop(0, members)
    def _(j):
        wu = u_of(j) * (1.0 / SUBGRID)
        wv = v_of(j) * (1.0 / SUBGRID)
        step_v = tuple(jnp.broadcast_to(t, (BLOCK, lanes)) for t in cis(turns(float(BLOCK), wv)))
        step_u = tuple(jnp.broadcast_to(t, (BLOCK, lanes)) for t in cis(turns(float(BLOCK), wu)))
        for b in range(across):
            k = (lines + (first_col + b * stride)).astype(jnp.float32)
            now = cis(turns(k, wv))
            for h in range(side // BLOCK):
                at = b * ALIGNED + h * BLOCK
                rhs[at : at + BLOCK, :lanes] = now[0].astype(jnp.bfloat16)
                rhs[at : at + BLOCK, lanes:] = (-now[1]).astype(jnp.bfloat16)
                now = cmul(now, step_v)
        total_r = jnp.zeros((BLOCK, lanes), jnp.float32)
        total_i = jnp.zeros((BLOCK, lanes), jnp.float32)
        for a in range(down):
            for b in range(across):
                for part in range(2):
                    cs[a, part * side : (part + 1) * side, b * ALIGNED : b * ALIGNED + side] = c_ref[
                        a * across + b, j, part
                    ]
            res = jnp.dot(cs[a], rhs[...], preferred_element_type=jnp.float32)
            k = (lines + (first_row + a * stride)).astype(jnp.float32)
            now = cis(turns(k, wu))
            for h in range(side // BLOCK):
                top = res[h * BLOCK : (h + 1) * BLOCK]
                low = res[side + h * BLOCK : side + (h + 1) * BLOCK]
                inner_r = top[:, :lanes] - low[:, lanes:]
                inner_i = top[:, lanes:] + low[:, :lanes]
                total_r = total_r + (now[0] * inner_r + now[1] * inner_i)
                total_i = total_i + (now[0] * inner_i - now[1] * inner_r)
                now = cmul(now, step_u)
        put(
            j,
            jnp.sum(total_r, axis=0, keepdims=True) * (1.0 / SUBGRID),
            jnp.sum(total_i, axis=0, keepdims=True) * (1.0 / SUBGRID),
        )


def model_kernel(per_group, c_ref, uv_ref, out_ref, cs, rhs):
    facet_here = lax.axis_index("facet")

    def put(j, real, imaginary):
        out_ref[j, 0:1, :] = real
        out_ref[j, 1:2, :] = imaginary

    partial_models(
        facet_here,
        per_group,
        c_ref,
        lambda j: uv_ref[j, 0:1, :],
        lambda j: uv_ref[j, 1:2, :],
        put,
        cs,
        rhs,
    )


def grid_kernel(per_group, side, gain, off_ref, all_ref, out_ref, acc, left, right):
    columns, depth, lanes = all_ref.shape
    members = depth // 4
    rows = out_ref.shape[2]
    stride = (SUBGRID - side) // (FACET_SIDE - 1)
    span = right.shape[0]
    facet_here = lax.axis_index("facet")
    first_line = lax.axis_index("sub") * rows
    facet_rows = -(-per_group // 8) * 8
    corner_r, corner_c = corner(row_iota(facet_rows, lanes) + facet_here * per_group, stride)
    lines8 = row_iota(8, lanes)
    lines = row_iota(BLOCK, lanes)
    acc[...] = jnp.zeros_like(acc)

    def wide(x, n):
        return tuple(jnp.broadcast_to(t, (n, lanes)) for t in x)

    def line(x, at):
        return tuple(t[at : at + 1] for t in x)

    def join(x, step):
        y = cmul(x, step)
        return tuple(jnp.concatenate([p, q], axis=0) for p, q in zip(x, y))

    @pl.loop(0, columns * members)
    def _(s):
        column = lax.div(s, members)
        j = lax.rem(s, members)
        off_r = off_ref[column, j, 0]
        off_c = off_ref[column, j, 1]
        start = lax.rem(first_line - off_r + WIN, WIN)
        start = jnp.where(start > WIN - rows, start - WIN, start)
        tile = lax.div(off_c, BLOCK) * BLOCK
        shift = off_c - tile

        @pl.when(start < side)
        def _():
            wu = all_ref[column, pl.ds(j, 1), :] * (1.0 / SUBGRID)
            wv = all_ref[column, pl.ds(members + j, 1), :] * (1.0 / SUBGRID)
            rr = all_ref[column, pl.ds(2 * members + j, 1), :] * gain
            ri = all_ref[column, pl.ds(3 * members + j, 1), :] * gain
            lead = cis(
                turns((corner_r + start).astype(jnp.float32), wu)
                + turns((corner_c - shift).astype(jnp.float32), wv)
            )
            lead = cmul(lead, (rr, ri))
            jumps_u = cis(turns(((lines8 + 1) * 8).astype(jnp.float32), wu))
            jumps_v = cis(turns(((lines8 + 1) * 8).astype(jnp.float32), wv))
            base_u = cis(turns(lines8.astype(jnp.float32), wu))
            base_v = cis(turns(lines8.astype(jnp.float32), wv))

            now = join(base_v, wide(line(jumps_v, 0), 8))
            step = wide(line(jumps_v, 1), BLOCK)
            for h in range(span // BLOCK):
                cell = lines + (h * BLOCK - shift)
                live = (cell >= 0) & (cell < side)
                at = h * BLOCK
                right[at : at + BLOCK, :lanes] = jnp.where(live, now[0], 0.0).astype(jnp.bfloat16)
                right[at : at + BLOCK, lanes:] = jnp.where(live, now[1], 0.0).astype(jnp.bfloat16)
                now = cmul(now, step)

            tall = min(rows, BLOCK)
            now = base_u if tall == 8 else join(base_u, wide(line(jumps_u, 0), 8))
            step = wide(line(jumps_u, 0 if tall == 8 else 1), tall)
            ladder = row_iota(tall, lanes)
            for h in range(rows // tall):
                cell = ladder + (h * tall + start)
                live = (cell >= 0) & (cell < side)
                masked = tuple(jnp.where(live, t, 0.0) for t in now)
                for f in range(per_group):
                    value = cmul(masked, wide(line(lead, f), tall))
                    at = 2 * f * rows + h * tall
                    real = value[0].astype(jnp.bfloat16)
                    left[at : at + tall, :lanes] = real
                    left[at + rows : at + rows + tall, lanes:] = real
                    left[at + rows : at + rows + tall, :lanes] = value[1].astype(jnp.bfloat16)
                    left[at : at + tall, lanes:] = (-value[1]).astype(jnp.bfloat16)
                now = cmul(now, step)

            where = pl.ds(pl.multiple_of(tile, BLOCK), span)
            acc[where, :] += lax.dot_general(
                right[...],
                left[...],
                (((1,), (1,)), ((), ())),
                preferred_element_type=jnp.float32,
            )

    spill = acc.shape[0] - WIN
    acc[:spill, :] += acc[WIN:, :]
    folded = acc[:WIN, :].T
    for f in range(per_group):
        for part in range(2):
            at = (2 * f + part) * rows
            out_ref[f, part] = folded[at : at + rows]


def model_call(contributions, uv):
    per_group, members, _, side, _ = contributions.shape
    lanes = uv.shape[-1]
    across = min(per_group, FACET_SIDE)
    return pl.pallas_call(
        functools.partial(model_kernel, per_group),
        out_shape=jax.ShapeDtypeStruct((members, 2, lanes), jnp.float32),
        in_specs=[pl.BlockSpec(memory_space=pltpu.VMEM)] * 2,
        out_specs=pl.BlockSpec(memory_space=pltpu.VMEM),
        scratch_shapes=[
            pltpu.VMEM((per_group // across, 2 * side, across * ALIGNED), jnp.bfloat16),
            pltpu.VMEM((across * ALIGNED, 2 * lanes), jnp.bfloat16),
        ],
    )(contributions, uv)


def grid_call(offsets, gathered, per_group, side, rows, gain):
    lanes = gathered.shape[-1]
    span = side + BLOCK
    width = 2 * per_group * rows
    return pl.pallas_call(
        functools.partial(grid_kernel, per_group, side, gain),
        out_shape=jax.ShapeDtypeStruct((per_group, 2, rows, WIN), jnp.float32),
        in_specs=[
            pl.BlockSpec(memory_space=pltpu.SMEM),
            pl.BlockSpec(memory_space=pltpu.VMEM),
        ],
        out_specs=pl.BlockSpec(memory_space=pltpu.VMEM),
        scratch_shapes=[
            pltpu.VMEM((WIN + side, width), jnp.float32),
            pltpu.VMEM((width, 2 * lanes), jnp.bfloat16),
            pltpu.VMEM((span, 2 * lanes), jnp.bfloat16),
        ],
    )(offsets, gathered)


def body(contributions, slot_subgrid, vis_count, vis_uv, vis_obs, vis_weight, subgrid_offset):
    columns = lax.axis_size("sub")
    per_group, _, members, _, side, _ = contributions.shape
    lanes = vis_weight.shape[-1]
    slots = vis_weight.shape[2]
    packed = jnp.concatenate(
        [
            vis_uv[0, 0],
            vis_obs[0, 0],
            vis_weight[0, 0][:, None],
            jnp.broadcast_to(vis_count[0, 0].astype(jnp.float32)[:, None, None], (slots, 1, lanes)),
        ],
        axis=1,
    )
    packed = lax.all_gather(packed, "facet", axis=0, tiled=True)
    table = slot_subgrid[0].reshape(-1)
    picked = jnp.stack(
        [
            jnp.sum(jnp.where((table == j)[:, None, None], packed, 0.0), axis=0)
            for j in range(members)
        ]
    )
    part = model_call(contributions[:, 0], picked[:, :2])
    model = lax.psum(part, "facet")
    live = jnp.arange(lanes, dtype=jnp.float32)[None, None, :] < picked[:, 5:6]
    resid = jnp.where(live, picked[:, 4:5] * (picked[:, 2:4] - model), 0.0)
    resid = resid.astype(jnp.bfloat16).astype(jnp.float32)
    mine = jnp.concatenate([picked[:, 0], picked[:, 1], resid[:, 0], resid[:, 1]], axis=0)
    gathered = lax.all_gather(mine, "sub", axis=0)
    offsets = lax.all_gather(subgrid_offset[0], "sub", axis=0)
    gain = WIN / (side * math.sqrt(members * columns)) / math.sqrt(lanes)
    return grid_call(offsets, gathered, per_group, side, WIN // columns, gain)


def solution(mesh):
    placed = (
        P("facet", "sub", None, None, None, None),
        P("sub", None, None),
        P("facet", "sub", None),
        P("facet", "sub", None, None, None),
        P("facet", "sub", None, None, None),
        P("facet", "sub", None, None),
        P("sub", None, None),
    )
    return jax.shard_map(
        body, mesh=mesh, in_specs=placed, out_specs=P("facet", None, "sub", None), check_vma=False
    )
```

time: 504 us -> 77.3 us (0.15)
  waiting for transfers between devices: 211 us -> 0 us
  local copies, waits for them, and re-layouts: 154 us -> 0.96 us
  other arithmetic: 47.6 us -> 2.79 us
  Pallas kernels: 0 us -> 20.1 us
  between operations: 15.9 us -> 0.08 us
  loops' own time: 10.9 us -> 0 us
  starting transfers between devices: 9.81 us -> 0 us
    reduce_scatter x1 -> x0, waiting for transfers between devices: 179 us -> none  [body(): summed = lax.psum_scatter(window, 'sub', scatter_dimension=2, tiled=True)]
    dynamic_update_slice x2 -> x0, local copies, waits for them, and re-layouts: 53.1 us -> none  [place_piece(): lax.dynamic_update_slice(accum, current + pieces.astype(jnp.float32), cor...]
    scatter-add x1 -> x0, local copies, waits for them, and re-layouts: 40.5 us -> none  [fold_edges(): return upper[..., :WIN].at[..., :CONTRIB].add(upper[..., WIN:])]
    unnamed x1 -> x0, blocking collectives: 36 us -> none
    all_gather x3, blocking collectives: 13.2 us -> 48.3 us  [the longest x1 24.7 us: body(): offsets = lax.all_gather(subgrid_offset[0], 'sub', axis=0)]
    all_to_all x2 -> x0, waiting for transfers between devices: 32.2 us -> none  [the longest x1 32.2 us: body(): lax.all_to_all(returned, 'facet', split_axis=0, concat_axis=0, tiled=True)]
    slice x5 -> x1, local copies, waits for them, and re-layouts: 29.9 us -> 0.01 us  [body(): resid[:, 0]]
    pallas_call x0 -> x2, Pallas kernels: none -> 20.1 us  [the longest x1 14 us: grid_call(): pl.pallas_call(functools.partial(grid_kernel, per_group, side, gain), out...]
  transfers between devices with their start and end apart: 3 -> 0, of which waited for: 2 -> 0; matrix products, arithmetic and copies ran while one was open for 1% -> 0% of each run, Pallas kernels for 0% -> 0%
where the time goes in v1:
time: 77.3 us
  blocking collectives  53.4 us (69%)
  Pallas kernels  20.1 us (26%)
  other arithmetic  2.79 us (4%)
  local copies, waits for them, and re-layouts  0.96 us (1%)
    all_gather x1, blocking collectives, body(): offsets = lax.all_gather(subgrid_offset[0], 'sub', axis=0)  24.7 us
    all_gather x1, blocking collectives, body(): gathered = lax.all_gather(mine, 'sub', axis=0)  19.1 us
    pallas_call x1, Pallas kernels, grid_call(): pl.pallas_call(functools.partial(grid_kernel, per_group, side, gain), out...  14 us
    pallas_call x1, Pallas kernels, model_call(): pl.pallas_call(functools.partial(model_kernel, per_group), out_shape=jax....  6.08 us
    psum x1, blocking collectives, body(): model = lax.psum(part, 'facet')  5.09 us
    all_gather x1, blocking collectives, body(): packed = lax.all_gather(packed, 'facet', axis=0, tiled=True)  4.5 us

profile of v1, /device:TPU:0, one launch (start us, length us, event | category | flops | bytes accessed | tf_op | source)
XLA Modules:
  0.0 77.3 jit_solution(9332389516923934938)
XLA Ops:
  0.0 0.7 convert_bitcast_fusion
  0.7 0.7 broadcast_compare_fusion
  1.3 0.1 eq.23
  1.4 0.1 eq.21
  1.5 0.1 broadcast_in_dim.42
  1.6 0.7 broadcast_in_dim_squeeze.3
  2.3 24.7 %all_gather.12.off_ref = s32[16,2,2]{2,1,0:T(2,128)} all-gather(s32[1,2,2]{2,1,0:T(2,128)} %param.13), channel_id=1, replica_groups=mesh['facet'=2,'sub'=16] {'sub'}, dimensions={0}, use_global_device_ids=true | all-gather | bytes 272 | tf_op jit(solution)/shard_map/all_gather | solution.py:285
  27.0 0.7 pad_maximum_fusion
  27.7 4.5 %all_gather.13 = f32[4,6,384]{2,1,0:T(8,128)S(1)} all-gather(f32[2,6,384]{2,1,0:T(8,128)S(1)} %pad_maximum_fusion), channel_id=1, replica_groups=mesh['facet'=2,'sub'=16] {'facet'}, dimensions={0}, use_global_device_ids=true | all-gather | bytes 55296 | tf_op jit(solution)/shard_map/all_gather | solution.py:270
  32.2 0.1 select_reduce_fusion.1
  32.4 0.6 pad_maximum_fusion.2.uv_ref
  33.0 6.1 %shard_map.73 = f32[2,2,384]{2,1,0:T(2,128)} custom-call(bf16[8,2,2,192,192]{4,3,2,1,0:T(8,128)(2,1)} %bitcast.22, f32[2,2,384]{2,1,0:T(2,128)} %pad_maximum_fusion.2.uv_ref), custom_call_target="tpu_custom_call" | custom-call | tf_op jit(solution)/shard_map/pallas_call | solution.py:224
  39.0 5.1 %psum.7 = f32[2,2,384]{2,1,0:T(2,128)S(1)} all-reduce(f32[2,2,384]{2,1,0:T(2,128)} %shard_map.73), channel_id=1, replica_groups=mesh['facet'=2,'sub'=16] {'facet'}, use_global_device_ids=true, to_apply=%region_2.3 | all-reduce | flops 1536 | bytes 12288 | tf_op jit(solution)/shard_map/psum | solution.py:279
  44.2 19.1 %all-gather = f32[128,384]{1,0:T(8,128)} all-gather(f32[8,384]{1,0:T(8,128)S(1)} %pad_maximum_fusion.1), channel_id=2, replica_groups=mesh['facet'=2,'sub'=16] {'sub'}, dimensions={0}, use_global_device_ids=true | all-gather | bytes 208896 | tf_op jit(solution)/shard_map/all_gather | solution.py:284
  63.3 14.0 %shard_map.74 = f32[8,2,32,512]{3,2,1,0:T(8,128)} custom-call(s32[16,2,2]{2,1,0:T(2,128)} %all_gather.12.off_ref, f32[16,8,384]{2,1,0:T(8,128)} %bitcast.23), custom_call_target="tpu_custom_call" | custom-call | tf_op jit(solution)/shard_map/pallas_call | solution.py:240
  (9 shorter events, 0.1 us)
